TPU v7x, 512 devices: a whole 4x4x16 slice. The times are simulated.
512 devices in a mesh: src: 16 (over z_lo, core), tgt: 32 (over z_hi, y, x).
Axes of the slice: x: 4, y: 4, z: 16 (z_hi: 2, z_lo: 8; z = z_hi * 8 + z_lo), core: 2. Of those that a mesh axis runs over, the one named last changes fastest.
Arguments:
- src_feats: bfloat16 [32, 40960], P(None, ('src', 'tgt')), may hold values from -7 to 7
- src_factor: bfloat16 [16, 40960], P(None, ('src', 'tgt')), may hold values from 0.1 to 8
- tgt_feats: bfloat16 [32, 65536], P(None, ('tgt', 'src')), may hold values from -7 to 7
- tgt_factor: bfloat16 [16, 65536], P(None, ('tgt', 'src')), may hold values from 0.1 to 8
- rank_weight: float32 [16], replicated, may hold values from 0.5 to 4
Outputs:
- grad_src_feats: float32 [32, 40960], P(None, ('src', 'tgt'))
- grad_src_factor: float32 [16, 40960], P(None, ('src', 'tgt'))
- grad_tgt_feats: float32 [32, 65536], P(None, ('tgt', 'src'))
- grad_tgt_factor: float32 [16, 65536], P(None, ('tgt', 'src'))
All inputs are finite; a program needn't handle non-finite values.
Results may differ from a plain program's by a relative error of at most 0.0015.
Values may be sent and summed in bfloat16 or wider, within the bound.
No kernel may reach another device: no remote copies, remote signals or barrier semaphores. Data moves between devices by JAX's collectives and lax.ppermute only.
A program may use at most 64 MiB of HBM per device.

v0:
```python
import jax
import jax.numpy as jnp
from jax import lax
from jax.sharding import PartitionSpec as P


def tile_terms(src_x, src_q, tgt_y, scaled_r, inverse_g):
    sq_src = jnp.sum(jnp.square(src_x.astype(jnp.float32)), 0)
    sq_tgt = jnp.sum(jnp.square(tgt_y.astype(jnp.float32)), 0)
    inner_prod = jnp.dot(src_x.T, tgt_y, preferred_element_type=jnp.float32)
    distance = jnp.sqrt(sq_src[:, None] + sq_tgt[None, :] - 2.0 * inner_prod + 1.0)
    plan_tile = jnp.dot(src_q.T, scaled_r, preferred_element_type=jnp.float32)
    weight = (plan_tile / distance).astype(jnp.bfloat16)
    cost_bf = distance.astype(jnp.bfloat16)
    row_mass = jnp.sum(weight.astype(jnp.float32), 1)
    col_mass = jnp.sum(weight.astype(jnp.float32), 0)
    grad_x = src_x.astype(jnp.float32) * row_mass[None, :] - jnp.dot(
        tgt_y, weight.T, preferred_element_type=jnp.float32
    )
    grad_q = jnp.dot(scaled_r, cost_bf.T, preferred_element_type=jnp.float32)
    grad_y = tgt_y.astype(jnp.float32) * col_mass[None, :] - jnp.dot(
        src_x, weight, preferred_element_type=jnp.float32
    )
    grad_r = inverse_g[:, None] * jnp.dot(src_q, cost_bf, preferred_element_type=jnp.float32)
    return (jnp.concatenate([grad_x, grad_q], 0), jnp.concatenate([grad_y, grad_r], 0))


def block_size(count):
    for candidate in (512, 256, 128):
        return candidate
    return count


def local(src_feats, src_factor, tgt_feats, tgt_factor, rank_weight):
    feature_count = src_feats.shape[0]
    stacked_count = feature_count + src_factor.shape[0]
    inverse_g = 1.0 / rank_weight
    tgt_whole = lax.all_gather(
        jnp.concatenate([tgt_feats, tgt_factor], 0), "src", axis=1, tiled=True
    )
    tgt_points = tgt_whole[:feature_count]
    scaled_r = (tgt_whole[feature_count:].astype(jnp.float32) * inverse_g[:, None]).astype(
        jnp.bfloat16
    )
    col_count = tgt_points.shape[1]
    total_tgt = tgt_feats.shape[1] * lax.axis_size("src") * lax.axis_size("tgt")
    src_stack = jnp.concatenate([src_feats, src_factor], 0)
    src_whole = lax.all_gather(src_stack, "tgt", axis=1, tiled=True)
    row_count = src_whole.shape[1]
    block_rows = block_size(row_count)

    def advance(block_index, totals):
        src_acc, tgt_acc = totals
        offset = block_index * block_rows
        part = lax.dynamic_slice_in_dim(src_whole, offset, block_rows, 1)
        src_part, tgt_part = tile_terms(
            part[:feature_count], part[feature_count:], tgt_points, scaled_r, inverse_g
        )
        src_acc = lax.dynamic_update_slice_in_dim(src_acc, src_part, offset, 1)
        tgt_acc = tgt_acc + tgt_part
        return (src_acc, tgt_acc)

    src_start = jnp.zeros((stacked_count, row_count), jnp.float32)
    tgt_start = jnp.zeros((stacked_count, col_count), jnp.float32)
    src_terms, tgt_terms = lax.fori_loop(
        0, row_count // block_rows, advance, (src_start, tgt_start)
    )
    src_sum = lax.psum_scatter(src_terms, "tgt", scatter_dimension=1, tiled=True)
    tgt_sum = lax.psum_scatter(tgt_terms, "src", scatter_dimension=1, tiled=True)
    scale = 1.0 / total_tgt
    return (
        src_sum[:feature_count] * scale,
        src_sum[feature_count:] * scale,
        tgt_sum[:feature_count] * scale,
        tgt_sum[feature_count:] * scale,
    )


def solution(mesh):
    placed = (
        P(None, ("src", "tgt")),
        P(None, ("src", "tgt")),
        P(None, ("tgt", "src")),
        P(None, ("tgt", "src")),
        P(),
    )
    return jax.shard_map(
        local,
        mesh=mesh,
        in_specs=placed,
        out_specs=(
            P(None, ("src", "tgt")),
            P(None, ("src", "tgt")),
            P(None, ("tgt", "src")),
            P(None, ("tgt", "src")),
        ),
        check_vma=False,
    )
```

profile of v0, /device:TPU:32, one launch (start us, length us, event | category | flops | bytes accessed | tf_op | source)
XLA Modules:
  0.0 646.9 jit_solution(10596549005930550365)
XLA Ops:
  7.2 0.7 broadcast_divide_fusion
  7.9 0.7 pad_maximum_fusion
  8.6 31.1 %all_gather.7 = bf16[48,2048]{1,0:T(8,128)(2,1)S(1)} all-gather(bf16[48,128]{1,0:T(8,128)(2,1)S(1)} %pad_maximum_fusion), channel_id=1, replica_groups=mesh['src'=16,'tgt'=32] {'src'}, dimensions={1}, use_global_device_ids=true | all-gather | bytes 208896 | tf_op jit(solution)/shard_map/all_gather | solution.py:38
  39.8 0.7 maximum_bitcast_fusion
  40.5 160.2 %all-gather = bf16[32,80,48]{1,2,0:T(8,128)(2,1)S(1)} all-gather(bf16[1,80,48]{1,2,0:T(8,128)(2,1)S(1)} %maximum_bitcast_fusion), channel_id=1, replica_groups=mesh['src'=16,'tgt'=32] {'tgt'}, dimensions={0}, use_global_device_ids=true | all-gather | bytes 253440 | tf_op jit(solution)/shard_map/all_gather | solution.py:48
  201.4 29.4 %while.16 = (s32[]{:T(128)}, f32[48,2560]{1,0:T(8,128)S(1)}, f32[48,2048]{1,0:T(8,128)S(1)}, bf16[48,2560]{1,0:T(8,128)(2,1)S(1)}, bf16[16,2048]{1,0:T(8,128)(2,...) while((s32[]{:T(128)}, f32[48,2560]{1,0:T(8,128)S(1)}, ...), condition=%wide.region_5.0_spmd.clone, body=%wide.region_0.0_spmd.clone.sunk | while | flops 314362880 | bytes 25797348 | solution.py:65
  201.5 2.3 add_sqrt_fusion.2
  203.9 0.6 convolution_bitcast_fusion.3
  204.9 1.0 convert_reduce_fusion.3
  206.0 0.7 fusion.44
  207.4 2.3 add_sqrt_fusion.2
  210.8 1.0 convert_reduce_fusion.3
  211.8 0.7 fusion.44
  213.3 2.3 add_sqrt_fusion.2
  215.6 0.6 convolution_bitcast_fusion.3
  216.7 1.0 convert_reduce_fusion.3
  217.7 0.7 fusion.44
  219.2 2.3 add_sqrt_fusion.2
  221.5 0.6 convolution_bitcast_fusion.3
  222.6 1.0 convert_reduce_fusion.3
  223.6 0.7 fusion.44
  225.1 2.3 add_sqrt_fusion.2
  228.5 1.0 convert_reduce_fusion.3
  229.5 0.7 fusion.44
  230.9 0.7 copy-done
  231.7 1.5 copy.11
  233.2 88.0 %reduce-scatter.5.cloned.1.call-done = f32[48,128]{1,0:T(8,128)} async-done(((f32[48,2048]{1,0:T(8,128)}), f32[48,128]{1,0:T(8,128)}) %reduce-scatter.5.cloned.1.call-update) | async-done | bytes 24592 | tf_op jit(solution)/shard_map/reduce_scatter | solution.py:69
  321.2 1.3 slice_multiply_fusion.1
  322.5 1.3 slice_multiply_fusion
  323.8 313.2 %reduce-scatter.7.cloned.1.call-done = f32[80,48]{1,0:T(8,128)} async-done(((f32[2560,48]{1,0:T(8,128)}), f32[80,48]{1,0:T(8,128)}) %reduce-scatter.7.cloned.1.call-update) | async-done | bytes 15376
  637.0 0.9 slice.43
  637.9 0.8 copy.13
  (46 shorter events, 9.0 us)
Async XLA Ops:
  7.2 314.0 %reduce-scatter.5.cloned.1.call-start = ((), (), s32[]{:S(2)}) async-start(), calls=%async_computation.2 | async-start | bytes 417792 | tf_op jit(solution)/shard_map/reduce_scatter | solution.py:69
  230.8 0.8 copy-start
  231.6 405.4 %reduce-scatter.7.cloned.1.call-start = ((), (), s32[]{:S(2)}) async-start(), calls=%async_computation.3 | async-start | bytes 1351680
Sparse Core Ops, SparseCore 0:
  231.7 89.3 reduce-scatter.4
  324.2 312.7 reduce-scatter.6
where the time goes:
time: 647 us
  waiting for transfers between devices  401 us (62%)
  blocking collectives  191 us (30%)
  matrix products  28 us (4%)
  between operations  14.1 us (2%)
  other arithmetic  7.12 us (1%)
    unnamed x3, waiting for transfers between devices  313 us
    all_gather x1, blocking collectives, local(): src_whole = lax.all_gather(src_stack, 'tgt', axis=1, tiled=True)  160 us
    reduce_scatter x1, waiting for transfers between devices, local(): lax.psum_scatter(tgt_terms, 'src', scatter_dimension=1, tiled=True)  88 us
    all_gather x1, blocking collectives, local(): lax.all_gather(jnp.concatenate([tgt_feats, tgt_factor], 0), 'src', axis=1...  31.1 us
  transfers between devices with their start and end apart: 2, of which 2 were waited for; matrix products, arithmetic and copies ran while one was open for 1% of the time, Pallas kernels for 0%

commit v1 on v0

--- a/solution.py
+++ b/solution.py
@@ -35,8 +35,14 @@
     feature_count = src_feats.shape[0]
     stacked_count = feature_count + src_factor.shape[0]
     inverse_g = 1.0 / rank_weight
-    tgt_whole = lax.all_gather(
-        jnp.concatenate([tgt_feats, tgt_factor], 0), "src", axis=1, tiled=True
+    tgt_whole = jnp.concatenate(
+        lax.all_to_all(
+            jnp.stack([jnp.concatenate([tgt_feats, tgt_factor], 0)] * lax.axis_size("src")),
+            "src",
+            0,
+            0,
+        ),
+        axis=1,
     )
     tgt_points = tgt_whole[:feature_count]
     scaled_r = (tgt_whole[feature_count:].astype(jnp.float32) * inverse_g[:, None]).astype(

time: 647 us -> 628 us (0.971)
  blocking collectives: 191 us -> 158 us
  starting transfers between devices: 0.08 us -> 12.7 us
    all_gather x1 -> x0, blocking collectives: 31.1 us -> none  [local(): lax.all_gather(jnp.concatenate([tgt_feats, tgt_factor], 0), 'src', axis=1...]
    all_to_all x0 -> x1, starting transfers between devices: none -> 12.6 us  [local(): lax.all_to_all(jnp.stack([jnp.concatenate([tgt_feats, tgt_factor], 0)] *...]
  transfers between devices with their start and end apart: 2 -> 3, of which waited for: 2 -> 2; matrix products, arithmetic and copies ran while one was open for 1% -> 1% of each run, Pallas kernels for 0% -> 0%
where the time goes in v1:
time: 628 us; the launch traced here: 627 us
  waiting for transfers between devices  401 us (64%)
  blocking collectives  158 us (25%)
  matrix products  28 us (4%)
  between operations  14.1 us (2%)
  starting transfers between devices  12.7 us (2%)
  other arithmetic  7.13 us (1%)
    unnamed x3, waiting for transfers between devices  313 us
    all_gather x1, blocking collectives, local(): src_whole = lax.all_gather(src_stack, 'tgt', axis=1, tiled=True)  158 us
    reduce_scatter x1, waiting for transfers between devices, local(): lax.psum_scatter(tgt_terms, 'src', scatter_dimension=1, tiled=True)  88.5 us
    all_to_all x1, starting transfers between devices, local(): lax.all_to_all(jnp.stack([jnp.concatenate([tgt_feats, tgt_factor], 0)] *...  12.6 us
  transfers between devices with their start and end apart: 3, of which 2 were waited for; matrix products, arithmetic and copies ran while one was open for 1% of the time, Pallas kernels for 0%

profile of v1, /device:TPU:32, one launch (start us, length us, event | category | flops | bytes accessed | tf_op | source)
XLA Modules:
  0.0 627.1 jit_solution(2824988060228032084)
XLA Ops:
  7.2 0.7 pad_maximum_fusion
  7.9 0.7 stack.2
  8.6 12.6 %all-to-all-start = ((bf16[16,48,128]{2,1,0:T(8,128)(2,1)}), bf16[16,48,128]{2,1,0:T(8,128)(2,1)S(1)}, u32[]{:S(2)}, u32[]{:S(2)}) async-start(bf16[16,48,128]{2,1,0:T(8,128)(2,1)} %stack.2), calls=%async_computation | async-start | bytes 393216 | tf_op jit(solution)/shard_map/all_to_all | solution.py:39
  21.3 0.7 maximum_bitcast_fusion
  22.0 158.0 %all-gather = bf16[32,80,48]{1,2,0:T(8,128)(2,1)S(1)} all-gather(bf16[1,80,48]{1,2,0:T(8,128)(2,1)S(1)} %maximum_bitcast_fusion), channel_id=1, replica_groups=mesh['src'=16,'tgt'=32] {'tgt'}, dimensions={0}, use_global_device_ids=true | all-gather | bytes 253440 | tf_op jit(solution)/shard_map/all_gather | solution.py:54
  180.7 0.7 broadcast_divide_fusion
  181.5 29.4 %while.16 = (s32[]{:T(128)}, f32[48,2560]{1,0:T(8,128)S(1)}, f32[48,2048]{1,0:T(8,128)S(1)}, bf16[48,2560]{1,0:T(8,128)(2,1)S(1)}, bf16[16,2048]{1,0:T(8,128)(2,...) while((s32[]{:T(128)}, f32[48,2560]{1,0:T(8,128)S(1)}, ...), condition=%wide.region_5.0_spmd.clone, body=%wide.region_0.0_spmd.clone.sunk | while | flops 314362880 | bytes 25797348 | solution.py:71
  181.6 2.3 add_sqrt_fusion.2
  183.9 0.6 convolution_bitcast_fusion.3
  185.0 1.0 convert_reduce_fusion.3
  186.0 0.7 fusion.45
  187.5 2.3 add_sqrt_fusion.2
  189.8 0.6 convolution_bitcast_fusion.3
  190.9 1.0 convert_reduce_fusion.3
  191.9 0.7 fusion.45
  193.4 2.3 add_sqrt_fusion.2
  196.7 1.0 convert_reduce_fusion.3
  197.8 0.7 fusion.45
  199.2 2.3 add_sqrt_fusion.2
  202.6 1.0 convert_reduce_fusion.3
  203.6 0.7 fusion.45
  205.1 2.3 add_sqrt_fusion.2
  208.5 1.0 convert_reduce_fusion.3
  209.5 0.7 fusion.45
  210.9 0.7 copy-done
  211.7 1.5 copy.13
  213.2 88.5 %reduce-scatter.5.cloned.1.call-done = f32[48,128]{1,0:T(8,128)} async-done(((f32[48,2048]{1,0:T(8,128)}), f32[48,128]{1,0:T(8,128)}) %reduce-scatter.5.cloned.1.call-update) | async-done | bytes 24592 | tf_op jit(solution)/shard_map/reduce_scatter | solution.py:75
  301.7 1.3 slice_multiply_fusion.1
  303.0 1.3 slice_multiply_fusion
  304.4 312.9 %reduce-scatter.7.cloned.1.call-done = f32[80,48]{1,0:T(8,128)} async-done(((f32[2560,48]{1,0:T(8,128)}), f32[80,48]{1,0:T(8,128)}) %reduce-scatter.7.cloned.1.call-update) | async-done | bytes 15376
  617.3 0.9 slice.48
  618.1 0.8 copy.15
  (48 shorter events, 9.7 us)
Async XLA Ops:
  8.6 172.8 %all-to-all-start = ((bf16[16,48,128]{2,1,0:T(8,128)(2,1)}), bf16[16,48,128]{2,1,0:T(8,128)(2,1)S(1)}, u32[]{:S(2)}, u32[]{:S(2)}) async-start(bf16[16,48,128]{2,1,0:T(8,128)(2,1)} %stack.2), calls=%async_computation | async-start | bytes 393216 | tf_op jit(solution)/shard_map/all_to_all | solution.py:39
  21.2 280.5 %reduce-scatter.5.cloned.1.call-start = ((), (), s32[]{:S(2)}) async-start(), calls=%async_computation.3 | async-start | bytes 417792 | tf_op jit(solution)/shard_map/reduce_scatter | solution.py:75
  210.9 0.8 copy-start
  211.7 405.6 %reduce-scatter.7.cloned.1.call-start = ((), (), s32[]{:S(2)}) async-start(), calls=%async_computation.4 | async-start | bytes 1351680
Sparse Core Ops, SparseCore 0:
  211.8 89.8 reduce-scatter.4
  304.8 312.4 reduce-scatter.6
